TPU v7x, 512 devices: a whole 4x8x8 slice. The times are simulated.
512 devices in a mesh: seq: 32 (over x, z), exp: 16 (over y, core).
Axes of the slice: x: 4, y: 8, z: 8, core: 2. Of those that a mesh axis runs over, the one named last changes fastest.
Arguments:
- queries: bfloat16 [8192, 2048], P('seq', 'exp'), may hold values from -112 to 112
- key_rows: bfloat16 [8192, 2048], P('seq', 'exp'), may hold values from -4 to 4
- value_rows: bfloat16 [8192, 2048], P('seq', 'exp'), may hold values from -6 to 6
- out_grad: bfloat16 [8192, 2048], P('seq', 'exp'), may hold values from -6 to 6
- expert_ids: int32 [8192, 2], P('seq'), may hold values from 0 to 31, all different within a row
- gate_values: float32 [8192, 2], P('seq'), may hold values from 0.1 to 1
- alibi_slope: float32 [16], P('exp'), may hold values from 0.00012207031 to 0.1
- expert_in: bfloat16 [32, 2048, 4096], P('seq', None, 'exp'), may hold values from -0.125 to 0.125
- expert_out: bfloat16 [32, 4096, 2048], P('seq', 'exp'), may hold values from -0.09375 to 0.09375
Outputs:
- query_grad: bfloat16 [8192, 2048], P('seq', 'exp')
- key_grad: bfloat16 [8192, 2048], P('seq', 'exp')
- value_grad: bfloat16 [8192, 2048], P('seq', 'exp')
- expert_in_grad: bfloat16 [32, 2048, 4096], P('seq', None, 'exp')
- expert_out_grad: bfloat16 [32, 4096, 2048], P('seq', 'exp')
Inputs may be any that keep to these rules, and one draw needn't show every extreme that they name: `expert_ids`: each token names two different experts.
All inputs are finite; a program needn't handle non-finite values.
Results may differ from a plain program's by a relative error of at most 0.024.
Values may be sent and summed in bfloat16 or wider, within the bound.
A program may use at most 128 MiB of HBM per device.

v0:
```python
import jax
import jax.numpy as jnp
from jax import lax
from jax.sharding import PartitionSpec as P

HD = 128
WCH = 16


def shifted(block, axis, distance):
    devices = range(lax.axis_size(axis))
    route = [(i - distance, i) for i in devices if i - distance in devices]
    return lax.ppermute(block, axis, route)


def window_scores(query_heads, key_stack, slopes, seq_index, window):
    score_scale = HD ** (-0.5)
    block_len = query_heads.shape[0]
    raw_scores = (
        jnp.einsum("ihd,jhd->hij", query_heads, key_stack, preferred_element_type=jnp.float32)
        * score_scale
    )
    row_pos = lax.broadcasted_iota(jnp.int32, (block_len, key_stack.shape[0]), 0)
    col_pos = lax.broadcasted_iota(jnp.int32, (block_len, key_stack.shape[0]), 1)
    back_block = col_pos // block_len
    distance = row_pos - col_pos % block_len + back_block * block_len
    in_window = (distance >= 0) & (distance < window) & (seq_index - back_block >= 0)
    biased = raw_scores - slopes[:, None, None] * distance.astype(jnp.float32)[None]
    return jnp.where(in_window[None], biased, -jnp.inf)


def slot_routing(expert_ids, experts, capacity):
    flat_ids = jnp.concatenate([expert_ids[:, 0], expert_ids[:, 1]])
    entry_count = flat_ids.shape[0]
    expert_cols = lax.broadcasted_iota(jnp.int32, (entry_count, experts), 1)
    one_hot = (flat_ids[:, None] == expert_cols).astype(jnp.int32)
    before = jnp.cumsum(one_hot, axis=0) - one_hot
    position = jnp.sum(before * one_hot, axis=1)
    is_kept = position < capacity
    slot_index = flat_ids * capacity + position
    slot_rows = lax.broadcasted_iota(jnp.int32, (experts * capacity, entry_count), 0)
    return ((slot_rows == slot_index[None, :]) & is_kept[None, :]).astype(jnp.bfloat16)


def per_device(
    queries,
    key_rows,
    value_rows,
    out_grad,
    expert_ids,
    gate_values,
    alibi_slope,
    expert_in,
    expert_out,
):
    score_scale = HD ** (-0.5)
    block_len = queries.shape[0]
    features = queries.shape[1]
    head_count = features // HD
    seq_index = lax.axis_index("seq")
    stretches = WCH + 1
    window = WCH * block_len

    def relay_keys(step, carry):
        stack_keys, stack_values, current_keys, current_values = carry
        current_keys, current_values = shifted((current_keys, current_values), "seq", 1)
        stack_keys = lax.dynamic_update_index_in_dim(stack_keys, current_keys, step, 0)
        stack_values = lax.dynamic_update_index_in_dim(stack_values, current_values, step, 0)
        return (stack_keys, stack_values, current_keys, current_values)

    empty_stack = jnp.zeros((stretches, block_len, features), jnp.bfloat16)
    start_keys = lax.dynamic_update_index_in_dim(empty_stack, key_rows, 0, 0)
    start_values = lax.dynamic_update_index_in_dim(empty_stack, value_rows, 0, 0)
    key_stack, value_stack, unused_keys, unused_values = lax.fori_loop(
        1, stretches, relay_keys, (start_keys, start_values, key_rows, value_rows)
    )
    key_block = key_stack.reshape(stretches * block_len, head_count, HD)
    value_block = value_stack.reshape(stretches * block_len, head_count, HD)
    query_heads = queries.reshape(block_len, head_count, HD)
    scores = window_scores(query_heads, key_block, alibi_slope, seq_index, window)
    log_norm = jax.nn.logsumexp(scores, axis=2)
    probs_full = jnp.exp(scores - log_norm[:, :, None])
    weights = probs_full.astype(jnp.bfloat16)
    attn_heads = jnp.einsum(
        "hij,jhd->ihd", weights, value_block, preferred_element_type=jnp.float32
    ).astype(jnp.bfloat16)
    attn_out = attn_heads.reshape(block_len, features)
    experts = lax.axis_size("seq")
    capacity = 5 * block_len // (2 * experts)
    routing = slot_routing(expert_ids, experts, capacity)
    both_tokens = jnp.concatenate([attn_out, attn_out])
    scaled_grad = jnp.concatenate(
        [gate_values[:, 0:1] * out_grad, gate_values[:, 1:2] * out_grad]
    ).astype(jnp.bfloat16)
    send_tokens = jnp.dot(routing, both_tokens, preferred_element_type=jnp.float32).astype(
        jnp.bfloat16
    )
    send_grads = jnp.dot(routing, scaled_grad, preferred_element_type=jnp.float32).astype(
        jnp.bfloat16
    )
    recv_tokens, recv_grads = (
        lax.all_to_all(send_tokens, "seq", split_axis=0, concat_axis=0, tiled=True),
        lax.all_to_all(send_grads, "seq", split_axis=0, concat_axis=0, tiled=True),
    )
    weight_in = expert_in[0]
    weight_out = expert_out[0]
    full_tokens = lax.all_gather(recv_tokens, "exp", axis=1, tiled=True)
    pre_act = jnp.dot(full_tokens, weight_in, preferred_element_type=jnp.float32)
    full_grads = lax.all_gather(recv_grads, "exp", axis=1, tiled=True)
    logistic = jax.nn.sigmoid(pre_act)
    hidden = (pre_act * logistic).astype(jnp.bfloat16)
    through_out = lax.dot_general(
        full_grads, weight_out, (((1,), (1,)), ((), ())), preferred_element_type=jnp.float32
    )
    hidden_grad = (through_out * logistic * (1.0 + pre_act * (1.0 - logistic))).astype(jnp.bfloat16)
    out_weight_grad = lax.dot_general(
        hidden, full_grads, (((0,), (0,)), ((), ())), preferred_element_type=jnp.float32
    ).astype(jnp.bfloat16)
    in_weight_grad = lax.dot_general(
        full_tokens, hidden_grad, (((0,), (0,)), ((), ())), preferred_element_type=jnp.float32
    ).astype(jnp.bfloat16)
    back_rows = lax.psum_scatter(
        lax.dot_general(
            weight_in, hidden_grad, (((1,), (1,)), ((), ())), preferred_element_type=jnp.float32
        ).astype(jnp.bfloat16),
        "exp",
        scatter_dimension=0,
        tiled=True,
    )
    returned = lax.all_to_all(back_rows, "seq", split_axis=1, concat_axis=1, tiled=True)
    combined = lax.dot_general(
        routing, returned, (((0,), (1,)), ((), ())), preferred_element_type=jnp.float32
    )
    attn_grad = (out_grad.astype(jnp.float32) + combined[:block_len] + combined[block_len:]).astype(
        jnp.bfloat16
    )
    grad_heads = attn_grad.reshape(block_len, head_count, HD)
    row_delta = jnp.einsum(
        "ihd,ihd->hi", grad_heads, attn_heads, preferred_element_type=jnp.float32
    )
    dprob = jnp.einsum("ihd,jhd->hij", grad_heads, value_block, preferred_element_type=jnp.float32)
    dscore = (probs_full * (dprob - row_delta[:, :, None])).astype(jnp.bfloat16)
    query_grad = (
        jnp.einsum("hij,jhd->ihd", dscore, key_block, preferred_element_type=jnp.float32)
        * score_scale
    ).astype(jnp.bfloat16)
    key_parts = (
        jnp.einsum("hij,ihd->jhd", dscore, query_heads, preferred_element_type=jnp.float32)
        * score_scale
    ).reshape(stretches, block_len, features)
    value_parts = jnp.einsum(
        "hij,ihd->jhd", weights, grad_heads, preferred_element_type=jnp.float32
    ).reshape(stretches, block_len, features)

    def relay_grads(step, carry):
        key_acc, value_acc = carry
        key_acc, value_acc = (
            shifted(key_acc.astype(jnp.bfloat16), "seq", -1).astype(key_acc.dtype),
            shifted(value_acc.astype(jnp.bfloat16), "seq", -1).astype(value_acc.dtype),
        )
        index = stretches - 1 - step
        key_acc = key_acc + lax.dynamic_index_in_dim(key_parts, index, 0, keepdims=False)
        value_acc = value_acc + lax.dynamic_index_in_dim(value_parts, index, 0, keepdims=False)
        return (key_acc, value_acc)

    key_total, value_total = lax.fori_loop(
        1, stretches, relay_grads, (key_parts[stretches - 1], value_parts[stretches - 1])
    )
    key_grad = key_total.astype(jnp.bfloat16)
    value_grad = value_total.astype(jnp.bfloat16)
    return (
        query_grad.reshape(block_len, features),
        key_grad,
        value_grad,
        in_weight_grad[None],
        out_weight_grad[None],
    )


def solution(mesh):
    return jax.shard_map(
        per_device,
        mesh=mesh,
        in_specs=(
            P("seq", "exp"),
            P("seq", "exp"),
            P("seq", "exp"),
            P("seq", "exp"),
            P("seq", None),
            P("seq", None),
            P("exp"),
            P("seq", None, "exp"),
            P("seq", "exp", None),
        ),
        out_specs=(
            P("seq", "exp"),
            P("seq", "exp"),
            P("seq", "exp"),
            P("seq", None, "exp"),
            P("seq", "exp", None),
        ),
        check_vma=False,
    )
```

profile of v0, /device:TPU:2, one launch (start us, length us, event | category | flops | bytes accessed | tf_op | source)
XLA Modules:
  0.0 586.6 jit_solution(2084339012505833438)
XLA Ops:
  14.8 170.1 %while.36 = (s32[]{:T(128)}, bf16[17,256,128]{2,1,0:T(8,128)(2,1)S(1)}, bf16[17,256,128]{2,1,0:T(8,128)(2,1)S(1)}, bf16[256,128]{1,0:T(8,128)(2,1)S(1)}, bf16[25...) while((s32[]{:T(128)}, bf16[17,256,128]{2,1,0:T(8,128)(2,1)S(1)}, ...), condition=%wide.region_1.2_spmd, body=%wide.region_0.1_spmd.sunk | while | flops 5 | bytes 1048783 | solution.py:74
  14.8 4.3 collective-permute-start.1
  19.1 4.3 collective-permute-start
  23.4 4.6 collective-permute-done.1
  35.1 3.7 collective-permute-done.1
  42.1 3.8 collective-permute-start
  52.4 4.0 collective-permute-start
  62.6 3.7 collective-permute-start
  85.1 4.4 collective-permute-done.1
  95.3 4.4 collective-permute-done.1
  106.2 5.0 collective-permute-done.1
  117.0 4.4 collective-permute-done.1
  127.3 5.0 collective-permute-done.1
  137.5 4.8 collective-permute-done.1
  147.8 4.4 collective-permute-done.1
  158.0 4.4 collective-permute-done.1
  168.3 4.4 collective-permute-done.1
  178.5 4.4 collective-permute-done.1
  184.9 5.8 fusion.71
  194.7 15.8 %all_to_all.36 = bf16[32,20,128]{2,1,0:T(8,128)(2,1)} all-to-all(bf16[32,20,128]{2,1,0:T(8,128)(2,1)S(1)} %all_to_all.27), channel_id=1, replica_groups=mesh['seq'=32,'exp'=16] {'seq'}, dimensions={0} | all-to-all | bytes 327680 | tf_op jit(solution)/shard_map/all_to_all | solution.py:102
  215.3 15.9 %all_to_all.37 = bf16[32,20,128]{2,1,0:T(8,128)(2,1)} all-to-all(bf16[32,20,128]{2,1,0:T(8,128)(2,1)S(1)} %all_to_all.24), channel_id=1, replica_groups=mesh['seq'=32,'exp'=16] {'seq'}, dimensions={0} | all-to-all | bytes 327680 | tf_op jit(solution)/shard_map/all_to_all | solution.py:103
  232.9 22.8 %all-gather.5.cloned.1.call-done = bf16[640,2048]{1,0:T(8,128)(2,1)} async-done(((bf16[640,128]{1,0:T(8,128)(2,1)}), bf16[640,2048]{1,0:T(8,128)(2,1)}) %all-gather.5.cloned.1.call-update) | async-done | bytes 2621456 | tf_op jit(solution)/shard_map/all_gather | solution.py:107
  259.2 43.8 %all-gather.3.cloned.1.call-done = bf16[640,2048]{1,0:T(8,128)(2,1)} async-done(((bf16[640,128]{1,0:T(8,128)(2,1)}), bf16[640,2048]{1,0:T(8,128)(2,1)}) %all-gather.3.cloned.1.call-update) | async-done | bytes 2621456 | tf_op jit(solution)/shard_map/all_gather | solution.py:109
  309.2 4.4 copy.33
  313.6 4.0 fusion.14
  317.6 57.7 %reduce-scatter.4.cloned.1.call-done = bf16[128,640]{1,0:T(8,128)(2,1)} async-done(((bf16[2048,640]{1,0:T(8,128)(2,1)}), bf16[128,640]{1,0:T(8,128)(2,1)}) %reduce-scatter.4.cloned.1.call-update) | async-done | bytes 163856
  377.0 10.5 %all-to-all-start.2 = ((bf16[128,32,20]{0,2,1:T(8,128)(2,1)}), bf16[128,32,20]{0,2,1:T(8,128)(2,1)S(1)}, u32[]{:S(2)}, u32[]{:S(2)}) async-start(bf16[128,32,20]{0,2,1:T(8,128)(2,1)} %all_to_all.30), calls=%async_computation.2 | async-start | bytes 393216 | tf_op jit(solution)/shard_map/all_to_all | solution.py:130
  387.5 3.8 fusion.13
  391.3 5.7 all-to-all-done.2
  403.4 4.0 fusion.4
  412.9 166.5 %while.37 = (s32[]{:T(128)}, bf16[256,128]{1,0:T(8,128)(2,1)S(1)}, bf16[256,128]{1,0:T(8,128)(2,1)S(1)}, f32[17,256,128]{2,1,0:T(8,128)S(1)}, f32[17,256,128]{2,...) while((s32[]{:T(128)}, bf16[256,128]{1,0:T(8,128)(2,1)S(1)}, ...), condition=%wide.region_9.10_spmd, body=%wide.region_8.9_spmd.sunk | while | flops 196614 | bytes 1048803 | solution.py:166
  416.1 3.6 collective-permute-start.2
  422.3 5.7 collective-permute-start.3
  434.2 4.2 collective-permute-start.3
  444.6 4.0 collective-permute-start.3
  455.3 4.2 collective-permute-start.3
  465.7 4.0 collective-permute-start.3
  475.9 4.0 collective-permute-start.3
  486.2 4.0 collective-permute-start.3
  496.4 4.0 collective-permute-start.3
  506.6 4.0 collective-permute-start.3
  513.7 3.6 collective-permute-done.2
  517.3 3.6 collective-permute-start.3
  527.1 4.0 collective-permute-start.3
  537.3 4.6 collective-permute-start.3
  548.6 4.2 collective-permute-start.3
  559.0 4.0 collective-permute-start.3
  569.2 4.0 collective-permute-start.3
  (264 shorter events, 232.5 us)
Async XLA Ops:
  7.2 248.6 %all-gather.5.cloned.1.call-start = ((), (), s32[]{:S(2)}) async-start(), calls=%async_computation.5 | async-start | bytes 2785280 | tf_op jit(solution)/shard_map/all_gather | solution.py:107
  14.8 13.2 %collective-permute-start.1 = (bf16[256,128]{1,0:T(8,128)(2,1)S(1)}, bf16[256,128]{1,0:T(8,128)(2,1)S(1)}, u32[]{:S(2)}, u32[]{:S(2)}) collective-permute-start(bf16[256,128]{1,0:T(8,128)(2,1)S(1)} %get-tuple-element.375), channel_id=1, source_target_pairs={{0,16},{16,32},{32,48},{48,64},{64,80},{80,96},{96,112},{112,128},... | collective-permute-start | bytes 196616 | tf_op jit(solution)/shard_map/while/body/eval_jaxpr/ppermute | solution.py:13
  19.1 10.8 %collective-permute-start = (bf16[256,128]{1,0:T(8,128)(2,1)S(1)}, bf16[256,128]{1,0:T(8,128)(2,1)S(1)}, u32[]{:S(2)}, u32[]{:S(2)}) collective-permute-start(bf16[256,128]{1,0:T(8,128)(2,1)S(1)} %get-tuple-element.374), channel_id=1, source_target_pairs={{0,16},{16,32},{32,48},{48,64},{64,80},{80,96},{96,112},{112,128},... | collective-permute-start | bytes 196616 | tf_op jit(solution)/shard_map/while/body/eval_jaxpr/ppermute | solution.py:13
  30.0 8.9 %collective-permute-start.1 = (bf16[256,128]{1,0:T(8,128)(2,1)S(1)}, bf16[256,128]{1,0:T(8,128)(2,1)S(1)}, u32[]{:S(2)}, u32[]{:S(2)}) collective-permute-start(bf16[256,128]{1,0:T(8,128)(2,1)S(1)} %get-tuple-element.375), channel_id=1, source_target_pairs={{0,16},{16,32},{32,48},{48,64},{64,80},{80,96},{96,112},{112,128},... | collective-permute-start | bytes 196616 | tf_op jit(solution)/shard_map/while/body/eval_jaxpr/ppermute | solution.py:13
  31.9 8.3 %collective-permute-start = (bf16[256,128]{1,0:T(8,128)(2,1)S(1)}, bf16[256,128]{1,0:T(8,128)(2,1)S(1)}, u32[]{:S(2)}, u32[]{:S(2)}) collective-permute-start(bf16[256,128]{1,0:T(8,128)(2,1)S(1)} %get-tuple-element.374), channel_id=1, source_target_pairs={{0,16},{16,32},{32,48},{48,64},{64,80},{80,96},{96,112},{112,128},... | collective-permute-start | bytes 196616 | tf_op jit(solution)/shard_map/while/body/eval_jaxpr/ppermute | solution.py:13
  40.2 8.7 %collective-permute-start.1 = (bf16[256,128]{1,0:T(8,128)(2,1)S(1)}, bf16[256,128]{1,0:T(8,128)(2,1)S(1)}, u32[]{:S(2)}, u32[]{:S(2)}) collective-permute-start(bf16[256,128]{1,0:T(8,128)(2,1)S(1)} %get-tuple-element.375), channel_id=1, source_target_pairs={{0,16},{16,32},{32,48},{48,64},{64,80},{80,96},{96,112},{112,128},... | collective-permute-start | bytes 196616 | tf_op jit(solution)/shard_map/while/body/eval_jaxpr/ppermute | solution.py:13
  42.1 8.3 %collective-permute-start = (bf16[256,128]{1,0:T(8,128)(2,1)S(1)}, bf16[256,128]{1,0:T(8,128)(2,1)S(1)}, u32[]{:S(2)}, u32[]{:S(2)}) collective-permute-start(bf16[256,128]{1,0:T(8,128)(2,1)S(1)} %get-tuple-element.374), channel_id=1, source_target_pairs={{0,16},{16,32},{32,48},{48,64},{64,80},{80,96},{96,112},{112,128},... | collective-permute-start | bytes 196616 | tf_op jit(solution)/shard_map/while/body/eval_jaxpr/ppermute | solution.py:13
  50.5 8.3 %collective-permute-start.1 = (bf16[256,128]{1,0:T(8,128)(2,1)S(1)}, bf16[256,128]{1,0:T(8,128)(2,1)S(1)}, u32[]{:S(2)}, u32[]{:S(2)}) collective-permute-start(bf16[256,128]{1,0:T(8,128)(2,1)S(1)} %get-tuple-element.375), channel_id=1, source_target_pairs={{0,16},{16,32},{32,48},{48,64},{64,80},{80,96},{96,112},{112,128},... | collective-permute-start | bytes 196616 | tf_op jit(solution)/shard_map/while/body/eval_jaxpr/ppermute | solution.py:13
  52.4 8.3 %collective-permute-start = (bf16[256,128]{1,0:T(8,128)(2,1)S(1)}, bf16[256,128]{1,0:T(8,128)(2,1)S(1)}, u32[]{:S(2)}, u32[]{:S(2)}) collective-permute-start(bf16[256,128]{1,0:T(8,128)(2,1)S(1)} %get-tuple-element.374), channel_id=1, source_target_pairs={{0,16},{16,32},{32,48},{48,64},{64,80},{80,96},{96,112},{112,128},... | collective-permute-start | bytes 196616 | tf_op jit(solution)/shard_map/while/body/eval_jaxpr/ppermute | solution.py:13
  60.7 8.3 %collective-permute-start.1 = (bf16[256,128]{1,0:T(8,128)(2,1)S(1)}, bf16[256,128]{1,0:T(8,128)(2,1)S(1)}, u32[]{:S(2)}, u32[]{:S(2)}) collective-permute-start(bf16[256,128]{1,0:T(8,128)(2,1)S(1)} %get-tuple-element.375), channel_id=1, source_target_pairs={{0,16},{16,32},{32,48},{48,64},{64,80},{80,96},{96,112},{112,128},... | collective-permute-start | bytes 196616 | tf_op jit(solution)/shard_map/while/body/eval_jaxpr/ppermute | solution.py:13
  62.6 8.3 %collective-permute-start = (bf16[256,128]{1,0:T(8,128)(2,1)S(1)}, bf16[256,128]{1,0:T(8,128)(2,1)S(1)}, u32[]{:S(2)}, u32[]{:S(2)}) collective-permute-start(bf16[256,128]{1,0:T(8,128)(2,1)S(1)} %get-tuple-element.374), channel_id=1, source_target_pairs={{0,16},{16,32},{32,48},{48,64},{64,80},{80,96},{96,112},{112,128},... | collective-permute-start | bytes 196616 | tf_op jit(solution)/shard_map/while/body/eval_jaxpr/ppermute | solution.py:13
  71.0 8.3 %collective-permute-start.1 = (bf16[256,128]{1,0:T(8,128)(2,1)S(1)}, bf16[256,128]{1,0:T(8,128)(2,1)S(1)}, u32[]{:S(2)}, u32[]{:S(2)}) collective-permute-start(bf16[256,128]{1,0:T(8,128)(2,1)S(1)} %get-tuple-element.375), channel_id=1, source_target_pairs={{0,16},{16,32},{32,48},{48,64},{64,80},{80,96},{96,112},{112,128},... | collective-permute-start | bytes 196616 | tf_op jit(solution)/shard_map/while/body/eval_jaxpr/ppermute | solution.py:13
  72.9 8.3 %collective-permute-start = (bf16[256,128]{1,0:T(8,128)(2,1)S(1)}, bf16[256,128]{1,0:T(8,128)(2,1)S(1)}, u32[]{:S(2)}, u32[]{:S(2)}) collective-permute-start(bf16[256,128]{1,0:T(8,128)(2,1)S(1)} %get-tuple-element.374), channel_id=1, source_target_pairs={{0,16},{16,32},{32,48},{48,64},{64,80},{80,96},{96,112},{112,128},... | collective-permute-start | bytes 196616 | tf_op jit(solution)/shard_map/while/body/eval_jaxpr/ppermute | solution.py:13
  81.2 8.3 %collective-permute-start.1 = (bf16[256,128]{1,0:T(8,128)(2,1)S(1)}, bf16[256,128]{1,0:T(8,128)(2,1)S(1)}, u32[]{:S(2)}, u32[]{:S(2)}) collective-permute-start(bf16[256,128]{1,0:T(8,128)(2,1)S(1)} %get-tuple-element.375), channel_id=1, source_target_pairs={{0,16},{16,32},{32,48},{48,64},{64,80},{80,96},{96,112},{112,128},... | collective-permute-start | bytes 196616 | tf_op jit(solution)/shard_map/while/body/eval_jaxpr/ppermute | solution.py:13
  83.1 8.3 %collective-permute-start = (bf16[256,128]{1,0:T(8,128)(2,1)S(1)}, bf16[256,128]{1,0:T(8,128)(2,1)S(1)}, u32[]{:S(2)}, u32[]{:S(2)}) collective-permute-start(bf16[256,128]{1,0:T(8,128)(2,1)S(1)} %get-tuple-element.374), channel_id=1, source_target_pairs={{0,16},{16,32},{32,48},{48,64},{64,80},{80,96},{96,112},{112,128},... | collective-permute-start | bytes 196616 | tf_op jit(solution)/shard_map/while/body/eval_jaxpr/ppermute | solution.py:13
  91.5 8.3 %collective-permute-start.1 = (bf16[256,128]{1,0:T(8,128)(2,1)S(1)}, bf16[256,128]{1,0:T(8,128)(2,1)S(1)}, u32[]{:S(2)}, u32[]{:S(2)}) collective-permute-start(bf16[256,128]{1,0:T(8,128)(2,1)S(1)} %get-tuple-element.375), channel_id=1, source_target_pairs={{0,16},{16,32},{32,48},{48,64},{64,80},{80,96},{96,112},{112,128},... | collective-permute-start | bytes 196616 | tf_op jit(solution)/shard_map/while/body/eval_jaxpr/ppermute | solution.py:13
  93.4 8.9 %collective-permute-start = (bf16[256,128]{1,0:T(8,128)(2,1)S(1)}, bf16[256,128]{1,0:T(8,128)(2,1)S(1)}, u32[]{:S(2)}, u32[]{:S(2)}) collective-permute-start(bf16[256,128]{1,0:T(8,128)(2,1)S(1)} %get-tuple-element.374), channel_id=1, source_target_pairs={{0,16},{16,32},{32,48},{48,64},{64,80},{80,96},{96,112},{112,128},... | collective-permute-start | bytes 196616 | tf_op jit(solution)/shard_map/while/body/eval_jaxpr/ppermute | solution.py:13
  102.3 8.9 %collective-permute-start.1 = (bf16[256,128]{1,0:T(8,128)(2,1)S(1)}, bf16[256,128]{1,0:T(8,128)(2,1)S(1)}, u32[]{:S(2)}, u32[]{:S(2)}) collective-permute-start(bf16[256,128]{1,0:T(8,128)(2,1)S(1)} %get-tuple-element.375), channel_id=1, source_target_pairs={{0,16},{16,32},{32,48},{48,64},{64,80},{80,96},{96,112},{112,128},... | collective-permute-start | bytes 196616 | tf_op jit(solution)/shard_map/while/body/eval_jaxpr/ppermute | solution.py:13
  104.2 8.9 %collective-permute-start = (bf16[256,128]{1,0:T(8,128)(2,1)S(1)}, bf16[256,128]{1,0:T(8,128)(2,1)S(1)}, u32[]{:S(2)}, u32[]{:S(2)}) collective-permute-start(bf16[256,128]{1,0:T(8,128)(2,1)S(1)} %get-tuple-element.374), channel_id=1, source_target_pairs={{0,16},{16,32},{32,48},{48,64},{64,80},{80,96},{96,112},{112,128},... | collective-permute-start | bytes 196616 | tf_op jit(solution)/shard_map/while/body/eval_jaxpr/ppermute | solution.py:13
  113.2 8.3 %collective-permute-start.1 = (bf16[256,128]{1,0:T(8,128)(2,1)S(1)}, bf16[256,128]{1,0:T(8,128)(2,1)S(1)}, u32[]{:S(2)}, u32[]{:S(2)}) collective-permute-start(bf16[256,128]{1,0:T(8,128)(2,1)S(1)} %get-tuple-element.375), channel_id=1, source_target_pairs={{0,16},{16,32},{32,48},{48,64},{64,80},{80,96},{96,112},{112,128},... | collective-permute-start | bytes 196616 | tf_op jit(solution)/shard_map/while/body/eval_jaxpr/ppermute | solution.py:13
  115.1 8.3 %collective-permute-start = (bf16[256,128]{1,0:T(8,128)(2,1)S(1)}, bf16[256,128]{1,0:T(8,128)(2,1)S(1)}, u32[]{:S(2)}, u32[]{:S(2)}) collective-permute-start(bf16[256,128]{1,0:T(8,128)(2,1)S(1)} %get-tuple-element.374), channel_id=1, source_target_pairs={{0,16},{16,32},{32,48},{48,64},{64,80},{80,96},{96,112},{112,128},... | collective-permute-start | bytes 196616 | tf_op jit(solution)/shard_map/while/body/eval_jaxpr/ppermute | solution.py:13
  123.4 8.9 %collective-permute-start.1 = (bf16[256,128]{1,0:T(8,128)(2,1)S(1)}, bf16[256,128]{1,0:T(8,128)(2,1)S(1)}, u32[]{:S(2)}, u32[]{:S(2)}) collective-permute-start(bf16[256,128]{1,0:T(8,128)(2,1)S(1)} %get-tuple-element.375), channel_id=1, source_target_pairs={{0,16},{16,32},{32,48},{48,64},{64,80},{80,96},{96,112},{112,128},... | collective-permute-start | bytes 196616 | tf_op jit(solution)/shard_map/while/body/eval_jaxpr/ppermute | solution.py:13
  125.4 8.3 %collective-permute-start = (bf16[256,128]{1,0:T(8,128)(2,1)S(1)}, bf16[256,128]{1,0:T(8,128)(2,1)S(1)}, u32[]{:S(2)}, u32[]{:S(2)}) collective-permute-start(bf16[256,128]{1,0:T(8,128)(2,1)S(1)} %get-tuple-element.374), channel_id=1, source_target_pairs={{0,16},{16,32},{32,48},{48,64},{64,80},{80,96},{96,112},{112,128},... | collective-permute-start | bytes 196616 | tf_op jit(solution)/shard_map/while/body/eval_jaxpr/ppermute | solution.py:13
  133.7 8.7 %collective-permute-start.1 = (bf16[256,128]{1,0:T(8,128)(2,1)S(1)}, bf16[256,128]{1,0:T(8,128)(2,1)S(1)}, u32[]{:S(2)}, u32[]{:S(2)}) collective-permute-start(bf16[256,128]{1,0:T(8,128)(2,1)S(1)} %get-tuple-element.375), channel_id=1, source_target_pairs={{0,16},{16,32},{32,48},{48,64},{64,80},{80,96},{96,112},{112,128},... | collective-permute-start | bytes 196616 | tf_op jit(solution)/shard_map/while/body/eval_jaxpr/ppermute | solution.py:13
  135.6 8.3 %collective-permute-start = (bf16[256,128]{1,0:T(8,128)(2,1)S(1)}, bf16[256,128]{1,0:T(8,128)(2,1)S(1)}, u32[]{:S(2)}, u32[]{:S(2)}) collective-permute-start(bf16[256,128]{1,0:T(8,128)(2,1)S(1)} %get-tuple-element.374), channel_id=1, source_target_pairs={{0,16},{16,32},{32,48},{48,64},{64,80},{80,96},{96,112},{112,128},... | collective-permute-start | bytes 196616 | tf_op jit(solution)/shard_map/while/body/eval_jaxpr/ppermute | solution.py:13
  143.9 8.3 %collective-permute-start.1 = (bf16[256,128]{1,0:T(8,128)(2,1)S(1)}, bf16[256,128]{1,0:T(8,128)(2,1)S(1)}, u32[]{:S(2)}, u32[]{:S(2)}) collective-permute-start(bf16[256,128]{1,0:T(8,128)(2,1)S(1)} %get-tuple-element.375), channel_id=1, source_target_pairs={{0,16},{16,32},{32,48},{48,64},{64,80},{80,96},{96,112},{112,128},... | collective-permute-start | bytes 196616 | tf_op jit(solution)/shard_map/while/body/eval_jaxpr/ppermute | solution.py:13
  145.9 8.3 %collective-permute-start = (bf16[256,128]{1,0:T(8,128)(2,1)S(1)}, bf16[256,128]{1,0:T(8,128)(2,1)S(1)}, u32[]{:S(2)}, u32[]{:S(2)}) collective-permute-start(bf16[256,128]{1,0:T(8,128)(2,1)S(1)} %get-tuple-element.374), channel_id=1, source_target_pairs={{0,16},{16,32},{32,48},{48,64},{64,80},{80,96},{96,112},{112,128},... | collective-permute-start | bytes 196616 | tf_op jit(solution)/shard_map/while/body/eval_jaxpr/ppermute | solution.py:13
  154.2 8.3 %collective-permute-start.1 = (bf16[256,128]{1,0:T(8,128)(2,1)S(1)}, bf16[256,128]{1,0:T(8,128)(2,1)S(1)}, u32[]{:S(2)}, u32[]{:S(2)}) collective-permute-start(bf16[256,128]{1,0:T(8,128)(2,1)S(1)} %get-tuple-element.375), channel_id=1, source_target_pairs={{0,16},{16,32},{32,48},{48,64},{64,80},{80,96},{96,112},{112,128},... | collective-permute-start | bytes 196616 | tf_op jit(solution)/shard_map/while/body/eval_jaxpr/ppermute | solution.py:13
  156.1 8.3 %collective-permute-start = (bf16[256,128]{1,0:T(8,128)(2,1)S(1)}, bf16[256,128]{1,0:T(8,128)(2,1)S(1)}, u32[]{:S(2)}, u32[]{:S(2)}) collective-permute-start(bf16[256,128]{1,0:T(8,128)(2,1)S(1)} %get-tuple-element.374), channel_id=1, source_target_pairs={{0,16},{16,32},{32,48},{48,64},{64,80},{80,96},{96,112},{112,128},... | collective-permute-start | bytes 196616 | tf_op jit(solution)/shard_map/while/body/eval_jaxpr/ppermute | solution.py:13
  164.4 8.3 %collective-permute-start.1 = (bf16[256,128]{1,0:T(8,128)(2,1)S(1)}, bf16[256,128]{1,0:T(8,128)(2,1)S(1)}, u32[]{:S(2)}, u32[]{:S(2)}) collective-permute-start(bf16[256,128]{1,0:T(8,128)(2,1)S(1)} %get-tuple-element.375), channel_id=1, source_target_pairs={{0,16},{16,32},{32,48},{48,64},{64,80},{80,96},{96,112},{112,128},... | collective-permute-start | bytes 196616 | tf_op jit(solution)/shard_map/while/body/eval_jaxpr/ppermute | solution.py:13
  166.4 8.3 %collective-permute-start = (bf16[256,128]{1,0:T(8,128)(2,1)S(1)}, bf16[256,128]{1,0:T(8,128)(2,1)S(1)}, u32[]{:S(2)}, u32[]{:S(2)}) collective-permute-start(bf16[256,128]{1,0:T(8,128)(2,1)S(1)} %get-tuple-element.374), channel_id=1, source_target_pairs={{0,16},{16,32},{32,48},{48,64},{64,80},{80,96},{96,112},{112,128},... | collective-permute-start | bytes 196616 | tf_op jit(solution)/shard_map/while/body/eval_jaxpr/ppermute | solution.py:13
  174.7 8.3 %collective-permute-start.1 = (bf16[256,128]{1,0:T(8,128)(2,1)S(1)}, bf16[256,128]{1,0:T(8,128)(2,1)S(1)}, u32[]{:S(2)}, u32[]{:S(2)}) collective-permute-start(bf16[256,128]{1,0:T(8,128)(2,1)S(1)} %get-tuple-element.375), channel_id=1, source_target_pairs={{0,16},{16,32},{32,48},{48,64},{64,80},{80,96},{96,112},{112,128},... | collective-permute-start | bytes 196616 | tf_op jit(solution)/shard_map/while/body/eval_jaxpr/ppermute | solution.py:13
  176.6 8.3 %collective-permute-start = (bf16[256,128]{1,0:T(8,128)(2,1)S(1)}, bf16[256,128]{1,0:T(8,128)(2,1)S(1)}, u32[]{:S(2)}, u32[]{:S(2)}) collective-permute-start(bf16[256,128]{1,0:T(8,128)(2,1)S(1)} %get-tuple-element.374), channel_id=1, source_target_pairs={{0,16},{16,32},{32,48},{48,64},{64,80},{80,96},{96,112},{112,128},... | collective-permute-start | bytes 196616 | tf_op jit(solution)/shard_map/while/body/eval_jaxpr/ppermute | solution.py:13
  212.2 90.8 %all-gather.3.cloned.1.call-start = ((), (), s32[]{:S(2)}) async-start(), calls=%async_computation.4 | async-start | bytes 2785280 | tf_op jit(solution)/shard_map/all_gather | solution.py:109
  232.9 142.4 %reduce-scatter.4.cloned.1.call-start = ((), (), s32[]{:S(2)}) async-start(), calls=%async_computation.6 | async-start | bytes 2785280
  377.0 20.0 %all-to-all-start.2 = ((bf16[128,32,20]{0,2,1:T(8,128)(2,1)}), bf16[128,32,20]{0,2,1:T(8,128)(2,1)S(1)}, u32[]{:S(2)}, u32[]{:S(2)}) async-start(bf16[128,32,20]{0,2,1:T(8,128)(2,1)} %all_to_all.30), calls=%async_computation.2 | async-start | bytes 393216 | tf_op jit(solution)/shard_map/all_to_all | solution.py:130
  412.9 6.8 %collective-permute-start.3 = (bf16[256,128]{1,0:T(8,128)(2,1)S(1)}, bf16[256,128]{1,0:T(8,128)(2,1)S(1)}, u32[]{:S(2)}, u32[]{:S(2)}) collective-permute-start(bf16[256,128]{1,0:T(8,128)(2,1)S(1)} %get-tuple-element.398), channel_id=1, source_target_pairs={{16,0},{32,16},{48,32},{64,48},{80,64},{96,80},{112,96},{128,112},... | collective-permute-start | bytes 196616 | tf_op jit(solution)/shard_map/while/body/eval_jaxpr/ppermute | solution.py:13
  422.3 7.7 %collective-permute-start.3 = (bf16[256,128]{1,0:T(8,128)(2,1)S(1)}, bf16[256,128]{1,0:T(8,128)(2,1)S(1)}, u32[]{:S(2)}, u32[]{:S(2)}) collective-permute-start(bf16[256,128]{1,0:T(8,128)(2,1)S(1)} %get-tuple-element.398), channel_id=1, source_target_pairs={{16,0},{32,16},{48,32},{64,48},{80,64},{96,80},{112,96},{128,112},... | collective-permute-start | bytes 196616 | tf_op jit(solution)/shard_map/while/body/eval_jaxpr/ppermute | solution.py:13
  428.0 6.2 %collective-permute-start.2 = (bf16[256,128]{1,0:T(8,128)(2,1)S(1)}, bf16[256,128]{1,0:T(8,128)(2,1)S(1)}, u32[]{:S(2)}, u32[]{:S(2)}) collective-permute-start(bf16[256,128]{1,0:T(8,128)(2,1)S(1)} %get-tuple-element.397), channel_id=1, source_target_pairs={{16,0},{32,16},{48,32},{64,48},{80,64},{96,80},{112,96},{128,112},... | collective-permute-start | bytes 196616 | tf_op jit(solution)/shard_map/while/body/eval_jaxpr/ppermute | solution.py:13
  434.2 6.2 %collective-permute-start.3 = (bf16[256,128]{1,0:T(8,128)(2,1)S(1)}, bf16[256,128]{1,0:T(8,128)(2,1)S(1)}, u32[]{:S(2)}, u32[]{:S(2)}) collective-permute-start(bf16[256,128]{1,0:T(8,128)(2,1)S(1)} %get-tuple-element.398), channel_id=1, source_target_pairs={{16,0},{32,16},{48,32},{64,48},{80,64},{96,80},{112,96},{128,112},... | collective-permute-start | bytes 196616 | tf_op jit(solution)/shard_map/while/body/eval_jaxpr/ppermute | solution.py:13
  444.6 6.6 %collective-permute-start.3 = (bf16[256,128]{1,0:T(8,128)(2,1)S(1)}, bf16[256,128]{1,0:T(8,128)(2,1)S(1)}, u32[]{:S(2)}, u32[]{:S(2)}) collective-permute-start(bf16[256,128]{1,0:T(8,128)(2,1)S(1)} %get-tuple-element.398), channel_id=1, source_target_pairs={{16,0},{32,16},{48,32},{64,48},{80,64},{96,80},{112,96},{128,112},... | collective-permute-start | bytes 196616 | tf_op jit(solution)/shard_map/while/body/eval_jaxpr/ppermute | solution.py:13
  448.6 6.6 %collective-permute-start.2 = (bf16[256,128]{1,0:T(8,128)(2,1)S(1)}, bf16[256,128]{1,0:T(8,128)(2,1)S(1)}, u32[]{:S(2)}, u32[]{:S(2)}) collective-permute-start(bf16[256,128]{1,0:T(8,128)(2,1)S(1)} %get-tuple-element.397), channel_id=1, source_target_pairs={{16,0},{32,16},{48,32},{64,48},{80,64},{96,80},{112,96},{128,112},... | collective-permute-start | bytes 196616 | tf_op jit(solution)/shard_map/while/body/eval_jaxpr/ppermute | solution.py:13
  465.7 6.4 %collective-permute-start.3 = (bf16[256,128]{1,0:T(8,128)(2,1)S(1)}, bf16[256,128]{1,0:T(8,128)(2,1)S(1)}, u32[]{:S(2)}, u32[]{:S(2)}) collective-permute-start(bf16[256,128]{1,0:T(8,128)(2,1)S(1)} %get-tuple-element.398), channel_id=1, source_target_pairs={{16,0},{32,16},{48,32},{64,48},{80,64},{96,80},{112,96},{128,112},... | collective-permute-start | bytes 196616 | tf_op jit(solution)/shard_map/while/body/eval_jaxpr/ppermute | solution.py:13
  475.9 6.2 %collective-permute-start.3 = (bf16[256,128]{1,0:T(8,128)(2,1)S(1)}, bf16[256,128]{1,0:T(8,128)(2,1)S(1)}, u32[]{:S(2)}, u32[]{:S(2)}) collective-permute-start(bf16[256,128]{1,0:T(8,128)(2,1)S(1)} %get-tuple-element.398), channel_id=1, source_target_pairs={{16,0},{32,16},{48,32},{64,48},{80,64},{96,80},{112,96},{128,112},... | collective-permute-start | bytes 196616 | tf_op jit(solution)/shard_map/while/body/eval_jaxpr/ppermute | solution.py:13
  496.4 6.8 %collective-permute-start.3 = (bf16[256,128]{1,0:T(8,128)(2,1)S(1)}, bf16[256,128]{1,0:T(8,128)(2,1)S(1)}, u32[]{:S(2)}, u32[]{:S(2)}) collective-permute-start(bf16[256,128]{1,0:T(8,128)(2,1)S(1)} %get-tuple-element.398), channel_id=1, source_target_pairs={{16,0},{32,16},{48,32},{64,48},{80,64},{96,80},{112,96},{128,112},... | collective-permute-start | bytes 196616 | tf_op jit(solution)/shard_map/while/body/eval_jaxpr/ppermute | solution.py:13
  510.7 6.6 %collective-permute-start.2 = (bf16[256,128]{1,0:T(8,128)(2,1)S(1)}, bf16[256,128]{1,0:T(8,128)(2,1)S(1)}, u32[]{:S(2)}, u32[]{:S(2)}) collective-permute-start(bf16[256,128]{1,0:T(8,128)(2,1)S(1)} %get-tuple-element.397), channel_id=1, source_target_pairs={{16,0},{32,16},{48,32},{64,48},{80,64},{96,80},{112,96},{128,112},... | collective-permute-start | bytes 196616 | tf_op jit(solution)/shard_map/while/body/eval_jaxpr/ppermute | solution.py:13
  537.3 7.0 %collective-permute-start.3 = (bf16[256,128]{1,0:T(8,128)(2,1)S(1)}, bf16[256,128]{1,0:T(8,128)(2,1)S(1)}, u32[]{:S(2)}, u32[]{:S(2)}) collective-permute-start(bf16[256,128]{1,0:T(8,128)(2,1)S(1)} %get-tuple-element.398), channel_id=1, source_target_pairs={{16,0},{32,16},{48,32},{64,48},{80,64},{96,80},{112,96},{128,112},... | collective-permute-start | bytes 196616 | tf_op jit(solution)/shard_map/while/body/eval_jaxpr/ppermute | solution.py:13
  541.9 6.7 %collective-permute-start.2 = (bf16[256,128]{1,0:T(8,128)(2,1)S(1)}, bf16[256,128]{1,0:T(8,128)(2,1)S(1)}, u32[]{:S(2)}, u32[]{:S(2)}) collective-permute-start(bf16[256,128]{1,0:T(8,128)(2,1)S(1)} %get-tuple-element.397), channel_id=1, source_target_pairs={{16,0},{32,16},{48,32},{64,48},{80,64},{96,80},{112,96},{128,112},... | collective-permute-start | bytes 196616 | tf_op jit(solution)/shard_map/while/body/eval_jaxpr/ppermute | solution.py:13
  (30 other events, 405.7 us)
Sparse Core Ops, SparseCore 0:
  212.3 43.3 all-gather.4
  258.4 44.5 all-gather.2
  313.7 61.4 reduce-scatter.3
where the time goes:
time: 590 us; the launch traced here: 587 us
  waiting for transfers between devices  277 us (47%)
  starting transfers between devices  183 us (31%)
  matrix products  35.4 us (6%)
  blocking collectives  31.8 us (5%)
  local copies, waits for them, and re-layouts  21.9 us (4%)
  other arithmetic  21.3 us (4%)
  between operations  14.7 us (2%)
    ppermute x64, starting transfers between devices, shifted(): return lax.ppermute(block, axis, route)  173 us
    ppermute x64, waiting for transfers between devices, shifted(): return lax.ppermute(block, axis, route)  147 us
    unnamed x4, waiting for transfers between devices  57.7 us
    all_gather x1, waiting for transfers between devices, per_device(): full_grads = lax.all_gather(recv_grads, 'exp', axis=1, tiled=True)  43.8 us
    all_gather x1, waiting for transfers between devices, per_device(): full_tokens = lax.all_gather(recv_tokens, 'exp', axis=1, tiled=True)  22.8 us
    all_to_all x1, blocking collectives, per_device(): lax.all_to_all(send_grads, 'seq', split_axis=0, concat_axis=0, tiled=True)  15.9 us
    all_to_all x1, blocking collectives, per_device(): lax.all_to_all(send_tokens, 'seq', split_axis=0, concat_axis=0, tiled=True)  15.8 us
    add x16, other arithmetic, relay_grads(): value_acc + lax.dynamic_index_in_dim(value_parts, index, 0, keepdims=False)  14.7 us
  transfers between devices with their start and end apart: 68, of which 64 were waited for; matrix products, arithmetic and copies ran while one was open for 5% of the time, Pallas kernels for 0%

commit v1 on v0

--- a/solution.py
+++ b/solution.py
@@ -5,6 +5,22 @@
 
 HD = 128
 WCH = 16
+
+
+def ring_gather(x, axis, dim):
+    ways, here, step = (lax.axis_size(axis), lax.axis_index(axis), x.shape[dim])
+    shape = [n * ways if d == dim else n for d, n in enumerate(x.shape)]
+    full = lax.dynamic_update_slice_in_dim(jnp.zeros(shape, x.dtype), x, here * step, axis=dim)
+    going_up = going_down = x
+    for far in range(1, ways // 2 + 1):
+        going_up = lax.ppermute(going_up, axis, [(d, (d + 1) % ways) for d in range(ways)])
+        full = lax.dynamic_update_slice_in_dim(full, going_up, (here - far) % ways * step, axis=dim)
+        if 2 * far < ways:
+            going_down = lax.ppermute(going_down, axis, [(d, (d - 1) % ways) for d in range(ways)])
+            full = lax.dynamic_update_slice_in_dim(
+                full, going_down, (here + far) % ways * step, axis=dim
+            )
+    return full
 
 
 def shifted(block, axis, distance):
@@ -106,7 +122,7 @@
     weight_out = expert_out[0]
     full_tokens = lax.all_gather(recv_tokens, "exp", axis=1, tiled=True)
     pre_act = jnp.dot(full_tokens, weight_in, preferred_element_type=jnp.float32)
-    full_grads = lax.all_gather(recv_grads, "exp", axis=1, tiled=True)
+    full_grads = ring_gather(recv_grads, "exp", 1)
     logistic = jax.nn.sigmoid(pre_act)
     hidden = (pre_act * logistic).astype(jnp.bfloat16)
     through_out = lax.dot_general(

time: 590 us -> 577 us (0.978)
  waiting for transfers between devices: 277 us -> 241 us
  starting transfers between devices: 183 us -> 204 us
  local copies, waits for them, and re-layouts: 21.9 us -> 30.4 us
    all_gather x1 -> x0, waiting for transfers between devices: 43.8 us -> none  [per_device(): full_grads = lax.all_gather(recv_grads, 'exp', axis=1, tiled=True)]
    all_gather x1, waiting for transfers between devices: 22.8 us -> 0.01 us  [per_device(): full_tokens = lax.all_gather(recv_tokens, 'exp', axis=1, tiled=True)]
    ppermute x0 -> x15, starting transfers between devices: none -> 21.5 us  [the longest x7 21.5 us: ring_gather(): lax.ppermute(going_down, axis, [(d, (d - 1) % ways) for d in range(ways)])]
    ppermute x0 -> x15, waiting for transfers between devices: none -> 17 us  [the longest x8 16.4 us: ring_gather(): lax.ppermute(going_up, axis, [(d, (d + 1) % ways) for d in range(ways)])]
    ppermute x64, waiting for transfers between devices: 147 us -> 161 us  [shifted(): return lax.ppermute(block, axis, route)]
    dynamic_update_slice x0 -> x16, local copies, waits for them, and re-layouts: none -> 11.2 us  [the longest x8 5.65 us: ring_gather(): lax.dynamic_update_slice_in_dim(full, going_up, (here - far) % ways * ste...]
    unnamed x4 -> x3, waiting for transfers between devices: 57.7 us -> 57 us
  transfers between devices with their start and end apart: 68 -> 82, of which waited for: 64 -> 73; matrix products, arithmetic and copies ran while one was open for 5% -> 4% of each run, Pallas kernels for 0% -> 0%
where the time goes in v1:
time: 577 us; the launch traced here: 575 us
  waiting for transfers between devices  241 us (42%)
  starting transfers between devices  204 us (35%)
  matrix products  32.7 us (6%)
  local copies, waits for them, and re-layouts  30.4 us (5%)
  blocking collectives  30.3 us (5%)
  other arithmetic  19.6 us (3%)
  between operations  15.1 us (3%)
    ppermute x64, starting transfers between devices, shifted(): return lax.ppermute(block, axis, route)  172 us
    ppermute x64, waiting for transfers between devices, shifted(): return lax.ppermute(block, axis, route)  161 us
    unnamed x3, waiting for transfers between devices  57 us
    ppermute x7, starting transfers between devices, ring_gather(): lax.ppermute(going_down, axis, [(d, (d - 1) % ways) for d in range(ways)])  21.5 us
    ppermute x8, waiting for transfers between devices, ring_gather(): lax.ppermute(going_up, axis, [(d, (d + 1) % ways) for d in range(ways)])  16.4 us
    all_to_all x1, blocking collectives, per_device(): lax.all_to_all(send_tokens, 'seq', split_axis=0, concat_axis=0, tiled=True)  15.9 us
    add x16, other arithmetic, relay_grads(): value_acc + lax.dynamic_index_in_dim(value_parts, index, 0, keepdims=False)  14.7 us
    all_to_all x1, blocking collectives, per_device(): lax.all_to_all(send_grads, 'seq', split_axis=0, concat_axis=0, tiled=True)  14.4 us
  transfers between devices with their start and end apart: 82, of which 73 were waited for; matrix products, arithmetic and copies ran while one was open for 4% of the time, Pallas kernels for 0%

profile of v1, /device:TPU:2, one launch (start us, length us, event | category | flops | bytes accessed | tf_op | source)
XLA Modules:
  0.0 574.7 jit_solution(11461478918284558488)
XLA Ops:
  14.8 170.1 %while.36 = (s32[]{:T(128)}, bf16[17,256,128]{2,1,0:T(8,128)(2,1)S(1)}, bf16[17,256,128]{2,1,0:T(8,128)(2,1)S(1)}, bf16[256,128]{1,0:T(8,128)(2,1)S(1)}, bf16[25...) while((s32[]{:T(128)}, bf16[17,256,128]{2,1,0:T(8,128)(2,1)S(1)}, ...), condition=%wide.region_1.2_spmd, body=%wide.region_0.1_spmd.sunk | while | flops 5 | bytes 1048791 | solution.py:90
  14.8 4.3 collective-permute-start
  19.1 4.3 collective-permute-start.1
  23.4 4.6 collective-permute-done
  52.4 4.0 collective-permute-start.1
  85.1 4.4 collective-permute-done
  95.4 4.4 collective-permute-done
  106.2 5.0 collective-permute-done
  117.1 4.4 collective-permute-done
  127.3 5.0 collective-permute-done
  137.6 4.8 collective-permute-done
  147.8 4.4 collective-permute-done
  158.1 4.4 collective-permute-done
  168.3 4.4 collective-permute-done
  178.6 4.4 collective-permute-done
  185.0 6.0 %fusion.71 = (f32[256]{0:T(256)S(1)}, f32[256,4352]{0,1:T(8,128)S(1)}) fusion(f32[]{:T(128)} %bitcast.116, bf16[4352,128]{1,0:T(8,128)(2,1)S(1)} %bitcast.121, bf16[256,128]{1,0:T(8,128)(2,1)} %param.13, s32[]{:T(128)S(6)} %axis_index.23, s32[4352]{0:T(1024)} %get-tuple-element.295, s32[4352]{0:T(1024)} %get-tuple-element.298, ...), kind=kOutput, calls=%fused_computation.120 | convolution fusion | flops 304152320 | bytes 5715464 | tf_op jit(solution)/shard_map/ihd,jhd->hij/dot_general | solution.py:36
  193.5 15.9 %all_to_all.36 = bf16[32,20,128]{2,1,0:T(8,128)(2,1)S(1)} all-to-all(bf16[32,20,128]{2,1,0:T(8,128)(2,1)S(1)} %all_to_all.27), channel_id=1, replica_groups=mesh['seq'=32,'exp'=16] {'seq'}, dimensions={0} | all-to-all | bytes 327680 | tf_op jit(solution)/shard_map/all_to_all | solution.py:118
  210.8 14.4 %all_to_all.37 = bf16[32,20,128]{2,1,0:T(8,128)(2,1)S(1)} all-to-all(bf16[32,20,128]{2,1,0:T(8,128)(2,1)S(1)} %all_to_all.24), channel_id=1, replica_groups=mesh['seq'=32,'exp'=16] {'seq'}, dimensions={0} | all-to-all | bytes 327680 | tf_op jit(solution)/shard_map/all_to_all | solution.py:119
  271.5 4.5 collective-permute-done.18
  284.5 4.4 copy.33
  292.7 56.9 %reduce-scatter.4.cloned.1.call-done = bf16[128,640]{1,0:T(8,128)(2,1)} async-done(((bf16[2048,640]{1,0:T(8,128)(2,1)}), bf16[128,640]{1,0:T(8,128)(2,1)}) %reduce-scatter.4.cloned.1.call-update) | async-done | bytes 163856
  351.5 10.5 %all-to-all-start.2 = ((bf16[128,32,20]{0,2,1:T(8,128)(2,1)}), bf16[128,32,20]{0,2,1:T(8,128)(2,1)S(1)}, u32[]{:S(2)}, u32[]{:S(2)}) async-start(bf16[128,32,20]{0,2,1:T(8,128)(2,1)} %all_to_all.30), calls=%async_computation.2 | async-start | bytes 393216 | tf_op jit(solution)/shard_map/all_to_all | solution.py:146
  365.7 5.7 all-to-all-done.2
  372.1 4.6 convolution_bitcast_fusion
  386.8 180.4 %while.37 = (s32[]{:T(128)}, bf16[256,128]{1,0:T(8,128)(2,1)S(1)}, bf16[256,128]{1,0:T(8,128)(2,1)S(1)}, f32[17,256,128]{2,1,0:T(8,128)S(1)}, f32[17,256,128]{2,...) while((s32[]{:T(128)}, bf16[256,128]{1,0:T(8,128)(2,1)S(1)}, ...), condition=%wide.region_9.10_spmd, body=%wide.region_8.9_spmd.sunk | while | flops 196614 | bytes 1048803 | solution.py:182
  397.5 5.2 collective-permute-start.2
  404.7 4.2 collective-permute-done.3
  409.8 4.0 collective-permute-start.2
  416.0 4.0 collective-permute-done.3
  421.0 4.4 collective-permute-start.2
  427.3 4.5 collective-permute-done.3
  443.6 4.3 collective-permute-start.2
  449.9 4.2 collective-permute-done.3
  455.0 4.0 collective-permute-start.2
  461.2 4.0 collective-permute-done.3
  466.2 4.0 collective-permute-start.2
  472.3 4.0 collective-permute-done.3
  477.3 4.0 collective-permute-start.2
  488.4 4.0 collective-permute-start.2
  494.6 4.2 collective-permute-done.3
  521.8 4.1 collective-permute-start.2
  528.0 4.1 collective-permute-done.3
  533.0 4.2 collective-permute-start.2
  539.9 4.0 collective-permute-done.3
  544.8 4.2 collective-permute-start.2
  551.0 4.1 collective-permute-done.3
  556.1 4.0 collective-permute-start.2
  562.3 4.0 collective-permute-done.3
  (312 shorter events, 276.5 us)
Async XLA Ops:
  7.2 269.5 %all-gather.2.cloned.1.call-start = ((), (), s32[]{:S(2)}) async-start(), calls=%async_computation.4 | async-start | bytes 2785280 | tf_op jit(solution)/shard_map/all_gather | solution.py:123
  14.8 13.2 %collective-permute-start = (bf16[256,128]{1,0:T(8,128)(2,1)S(1)}, bf16[256,128]{1,0:T(8,128)(2,1)S(1)}, u32[]{:S(2)}, u32[]{:S(2)}) collective-permute-start(bf16[256,128]{1,0:T(8,128)(2,1)S(1)} %get-tuple-element.374), channel_id=1, source_target_pairs={{0,16},{16,32},{32,48},{48,64},{64,80},{80,96},{96,112},{112,128},... | collective-permute-start | bytes 196616 | tf_op jit(solution)/shard_map/while/body/eval_jaxpr/ppermute | solution.py:29
  19.1 10.8 %collective-permute-start.1 = (bf16[256,128]{1,0:T(8,128)(2,1)S(1)}, bf16[256,128]{1,0:T(8,128)(2,1)S(1)}, u32[]{:S(2)}, u32[]{:S(2)}) collective-permute-start(bf16[256,128]{1,0:T(8,128)(2,1)S(1)} %get-tuple-element.375), channel_id=1, source_target_pairs={{0,16},{16,32},{32,48},{48,64},{64,80},{80,96},{96,112},{112,128},... | collective-permute-start | bytes 196616 | tf_op jit(solution)/shard_map/while/body/eval_jaxpr/ppermute | solution.py:29
  30.0 8.9 %collective-permute-start = (bf16[256,128]{1,0:T(8,128)(2,1)S(1)}, bf16[256,128]{1,0:T(8,128)(2,1)S(1)}, u32[]{:S(2)}, u32[]{:S(2)}) collective-permute-start(bf16[256,128]{1,0:T(8,128)(2,1)S(1)} %get-tuple-element.374), channel_id=1, source_target_pairs={{0,16},{16,32},{32,48},{48,64},{64,80},{80,96},{96,112},{112,128},... | collective-permute-start | bytes 196616 | tf_op jit(solution)/shard_map/while/body/eval_jaxpr/ppermute | solution.py:29
  31.9 8.3 %collective-permute-start.1 = (bf16[256,128]{1,0:T(8,128)(2,1)S(1)}, bf16[256,128]{1,0:T(8,128)(2,1)S(1)}, u32[]{:S(2)}, u32[]{:S(2)}) collective-permute-start(bf16[256,128]{1,0:T(8,128)(2,1)S(1)} %get-tuple-element.375), channel_id=1, source_target_pairs={{0,16},{16,32},{32,48},{48,64},{64,80},{80,96},{96,112},{112,128},... | collective-permute-start | bytes 196616 | tf_op jit(solution)/shard_map/while/body/eval_jaxpr/ppermute | solution.py:29
  40.2 8.7 %collective-permute-start = (bf16[256,128]{1,0:T(8,128)(2,1)S(1)}, bf16[256,128]{1,0:T(8,128)(2,1)S(1)}, u32[]{:S(2)}, u32[]{:S(2)}) collective-permute-start(bf16[256,128]{1,0:T(8,128)(2,1)S(1)} %get-tuple-element.374), channel_id=1, source_target_pairs={{0,16},{16,32},{32,48},{48,64},{64,80},{80,96},{96,112},{112,128},... | collective-permute-start | bytes 196616 | tf_op jit(solution)/shard_map/while/body/eval_jaxpr/ppermute | solution.py:29
  42.2 8.3 %collective-permute-start.1 = (bf16[256,128]{1,0:T(8,128)(2,1)S(1)}, bf16[256,128]{1,0:T(8,128)(2,1)S(1)}, u32[]{:S(2)}, u32[]{:S(2)}) collective-permute-start(bf16[256,128]{1,0:T(8,128)(2,1)S(1)} %get-tuple-element.375), channel_id=1, source_target_pairs={{0,16},{16,32},{32,48},{48,64},{64,80},{80,96},{96,112},{112,128},... | collective-permute-start | bytes 196616 | tf_op jit(solution)/shard_map/while/body/eval_jaxpr/ppermute | solution.py:29
  50.5 8.3 %collective-permute-start = (bf16[256,128]{1,0:T(8,128)(2,1)S(1)}, bf16[256,128]{1,0:T(8,128)(2,1)S(1)}, u32[]{:S(2)}, u32[]{:S(2)}) collective-permute-start(bf16[256,128]{1,0:T(8,128)(2,1)S(1)} %get-tuple-element.374), channel_id=1, source_target_pairs={{0,16},{16,32},{32,48},{48,64},{64,80},{80,96},{96,112},{112,128},... | collective-permute-start | bytes 196616 | tf_op jit(solution)/shard_map/while/body/eval_jaxpr/ppermute | solution.py:29
  52.4 8.3 %collective-permute-start.1 = (bf16[256,128]{1,0:T(8,128)(2,1)S(1)}, bf16[256,128]{1,0:T(8,128)(2,1)S(1)}, u32[]{:S(2)}, u32[]{:S(2)}) collective-permute-start(bf16[256,128]{1,0:T(8,128)(2,1)S(1)} %get-tuple-element.375), channel_id=1, source_target_pairs={{0,16},{16,32},{32,48},{48,64},{64,80},{80,96},{96,112},{112,128},... | collective-permute-start | bytes 196616 | tf_op jit(solution)/shard_map/while/body/eval_jaxpr/ppermute | solution.py:29
  60.7 8.3 %collective-permute-start = (bf16[256,128]{1,0:T(8,128)(2,1)S(1)}, bf16[256,128]{1,0:T(8,128)(2,1)S(1)}, u32[]{:S(2)}, u32[]{:S(2)}) collective-permute-start(bf16[256,128]{1,0:T(8,128)(2,1)S(1)} %get-tuple-element.374), channel_id=1, source_target_pairs={{0,16},{16,32},{32,48},{48,64},{64,80},{80,96},{96,112},{112,128},... | collective-permute-start | bytes 196616 | tf_op jit(solution)/shard_map/while/body/eval_jaxpr/ppermute | solution.py:29
  62.7 8.3 %collective-permute-start.1 = (bf16[256,128]{1,0:T(8,128)(2,1)S(1)}, bf16[256,128]{1,0:T(8,128)(2,1)S(1)}, u32[]{:S(2)}, u32[]{:S(2)}) collective-permute-start(bf16[256,128]{1,0:T(8,128)(2,1)S(1)} %get-tuple-element.375), channel_id=1, source_target_pairs={{0,16},{16,32},{32,48},{48,64},{64,80},{80,96},{96,112},{112,128},... | collective-permute-start | bytes 196616 | tf_op jit(solution)/shard_map/while/body/eval_jaxpr/ppermute | solution.py:29
  71.0 8.3 %collective-permute-start = (bf16[256,128]{1,0:T(8,128)(2,1)S(1)}, bf16[256,128]{1,0:T(8,128)(2,1)S(1)}, u32[]{:S(2)}, u32[]{:S(2)}) collective-permute-start(bf16[256,128]{1,0:T(8,128)(2,1)S(1)} %get-tuple-element.374), channel_id=1, source_target_pairs={{0,16},{16,32},{32,48},{48,64},{64,80},{80,96},{96,112},{112,128},... | collective-permute-start | bytes 196616 | tf_op jit(solution)/shard_map/while/body/eval_jaxpr/ppermute | solution.py:29
  72.9 8.3 %collective-permute-start.1 = (bf16[256,128]{1,0:T(8,128)(2,1)S(1)}, bf16[256,128]{1,0:T(8,128)(2,1)S(1)}, u32[]{:S(2)}, u32[]{:S(2)}) collective-permute-start(bf16[256,128]{1,0:T(8,128)(2,1)S(1)} %get-tuple-element.375), channel_id=1, source_target_pairs={{0,16},{16,32},{32,48},{48,64},{64,80},{80,96},{96,112},{112,128},... | collective-permute-start | bytes 196616 | tf_op jit(solution)/shard_map/while/body/eval_jaxpr/ppermute | solution.py:29
  81.2 8.3 %collective-permute-start = (bf16[256,128]{1,0:T(8,128)(2,1)S(1)}, bf16[256,128]{1,0:T(8,128)(2,1)S(1)}, u32[]{:S(2)}, u32[]{:S(2)}) collective-permute-start(bf16[256,128]{1,0:T(8,128)(2,1)S(1)} %get-tuple-element.374), channel_id=1, source_target_pairs={{0,16},{16,32},{32,48},{48,64},{64,80},{80,96},{96,112},{112,128},... | collective-permute-start | bytes 196616 | tf_op jit(solution)/shard_map/while/body/eval_jaxpr/ppermute | solution.py:29
  83.2 8.3 %collective-permute-start.1 = (bf16[256,128]{1,0:T(8,128)(2,1)S(1)}, bf16[256,128]{1,0:T(8,128)(2,1)S(1)}, u32[]{:S(2)}, u32[]{:S(2)}) collective-permute-start(bf16[256,128]{1,0:T(8,128)(2,1)S(1)} %get-tuple-element.375), channel_id=1, source_target_pairs={{0,16},{16,32},{32,48},{48,64},{64,80},{80,96},{96,112},{112,128},... | collective-permute-start | bytes 196616 | tf_op jit(solution)/shard_map/while/body/eval_jaxpr/ppermute | solution.py:29
  91.5 8.3 %collective-permute-start = (bf16[256,128]{1,0:T(8,128)(2,1)S(1)}, bf16[256,128]{1,0:T(8,128)(2,1)S(1)}, u32[]{:S(2)}, u32[]{:S(2)}) collective-permute-start(bf16[256,128]{1,0:T(8,128)(2,1)S(1)} %get-tuple-element.374), channel_id=1, source_target_pairs={{0,16},{16,32},{32,48},{48,64},{64,80},{80,96},{96,112},{112,128},... | collective-permute-start | bytes 196616 | tf_op jit(solution)/shard_map/while/body/eval_jaxpr/ppermute | solution.py:29
  93.4 8.9 %collective-permute-start.1 = (bf16[256,128]{1,0:T(8,128)(2,1)S(1)}, bf16[256,128]{1,0:T(8,128)(2,1)S(1)}, u32[]{:S(2)}, u32[]{:S(2)}) collective-permute-start(bf16[256,128]{1,0:T(8,128)(2,1)S(1)} %get-tuple-element.375), channel_id=1, source_target_pairs={{0,16},{16,32},{32,48},{48,64},{64,80},{80,96},{96,112},{112,128},... | collective-permute-start | bytes 196616 | tf_op jit(solution)/shard_map/while/body/eval_jaxpr/ppermute | solution.py:29
  102.3 8.9 %collective-permute-start = (bf16[256,128]{1,0:T(8,128)(2,1)S(1)}, bf16[256,128]{1,0:T(8,128)(2,1)S(1)}, u32[]{:S(2)}, u32[]{:S(2)}) collective-permute-start(bf16[256,128]{1,0:T(8,128)(2,1)S(1)} %get-tuple-element.374), channel_id=1, source_target_pairs={{0,16},{16,32},{32,48},{48,64},{64,80},{80,96},{96,112},{112,128},... | collective-permute-start | bytes 196616 | tf_op jit(solution)/shard_map/while/body/eval_jaxpr/ppermute | solution.py:29
  104.3 8.9 %collective-permute-start.1 = (bf16[256,128]{1,0:T(8,128)(2,1)S(1)}, bf16[256,128]{1,0:T(8,128)(2,1)S(1)}, u32[]{:S(2)}, u32[]{:S(2)}) collective-permute-start(bf16[256,128]{1,0:T(8,128)(2,1)S(1)} %get-tuple-element.375), channel_id=1, source_target_pairs={{0,16},{16,32},{32,48},{48,64},{64,80},{80,96},{96,112},{112,128},... | collective-permute-start | bytes 196616 | tf_op jit(solution)/shard_map/while/body/eval_jaxpr/ppermute | solution.py:29
  113.2 8.3 %collective-permute-start = (bf16[256,128]{1,0:T(8,128)(2,1)S(1)}, bf16[256,128]{1,0:T(8,128)(2,1)S(1)}, u32[]{:S(2)}, u32[]{:S(2)}) collective-permute-start(bf16[256,128]{1,0:T(8,128)(2,1)S(1)} %get-tuple-element.374), channel_id=1, source_target_pairs={{0,16},{16,32},{32,48},{48,64},{64,80},{80,96},{96,112},{112,128},... | collective-permute-start | bytes 196616 | tf_op jit(solution)/shard_map/while/body/eval_jaxpr/ppermute | solution.py:29
  115.1 8.3 %collective-permute-start.1 = (bf16[256,128]{1,0:T(8,128)(2,1)S(1)}, bf16[256,128]{1,0:T(8,128)(2,1)S(1)}, u32[]{:S(2)}, u32[]{:S(2)}) collective-permute-start(bf16[256,128]{1,0:T(8,128)(2,1)S(1)} %get-tuple-element.375), channel_id=1, source_target_pairs={{0,16},{16,32},{32,48},{48,64},{64,80},{80,96},{96,112},{112,128},... | collective-permute-start | bytes 196616 | tf_op jit(solution)/shard_map/while/body/eval_jaxpr/ppermute | solution.py:29
  123.5 8.9 %collective-permute-start = (bf16[256,128]{1,0:T(8,128)(2,1)S(1)}, bf16[256,128]{1,0:T(8,128)(2,1)S(1)}, u32[]{:S(2)}, u32[]{:S(2)}) collective-permute-start(bf16[256,128]{1,0:T(8,128)(2,1)S(1)} %get-tuple-element.374), channel_id=1, source_target_pairs={{0,16},{16,32},{32,48},{48,64},{64,80},{80,96},{96,112},{112,128},... | collective-permute-start | bytes 196616 | tf_op jit(solution)/shard_map/while/body/eval_jaxpr/ppermute | solution.py:29
  125.4 8.3 %collective-permute-start.1 = (bf16[256,128]{1,0:T(8,128)(2,1)S(1)}, bf16[256,128]{1,0:T(8,128)(2,1)S(1)}, u32[]{:S(2)}, u32[]{:S(2)}) collective-permute-start(bf16[256,128]{1,0:T(8,128)(2,1)S(1)} %get-tuple-element.375), channel_id=1, source_target_pairs={{0,16},{16,32},{32,48},{48,64},{64,80},{80,96},{96,112},{112,128},... | collective-permute-start | bytes 196616 | tf_op jit(solution)/shard_map/while/body/eval_jaxpr/ppermute | solution.py:29
  133.7 8.7 %collective-permute-start = (bf16[256,128]{1,0:T(8,128)(2,1)S(1)}, bf16[256,128]{1,0:T(8,128)(2,1)S(1)}, u32[]{:S(2)}, u32[]{:S(2)}) collective-permute-start(bf16[256,128]{1,0:T(8,128)(2,1)S(1)} %get-tuple-element.374), channel_id=1, source_target_pairs={{0,16},{16,32},{32,48},{48,64},{64,80},{80,96},{96,112},{112,128},... | collective-permute-start | bytes 196616 | tf_op jit(solution)/shard_map/while/body/eval_jaxpr/ppermute | solution.py:29
  135.6 8.3 %collective-permute-start.1 = (bf16[256,128]{1,0:T(8,128)(2,1)S(1)}, bf16[256,128]{1,0:T(8,128)(2,1)S(1)}, u32[]{:S(2)}, u32[]{:S(2)}) collective-permute-start(bf16[256,128]{1,0:T(8,128)(2,1)S(1)} %get-tuple-element.375), channel_id=1, source_target_pairs={{0,16},{16,32},{32,48},{48,64},{64,80},{80,96},{96,112},{112,128},... | collective-permute-start | bytes 196616 | tf_op jit(solution)/shard_map/while/body/eval_jaxpr/ppermute | solution.py:29
  144.0 8.3 %collective-permute-start = (bf16[256,128]{1,0:T(8,128)(2,1)S(1)}, bf16[256,128]{1,0:T(8,128)(2,1)S(1)}, u32[]{:S(2)}, u32[]{:S(2)}) collective-permute-start(bf16[256,128]{1,0:T(8,128)(2,1)S(1)} %get-tuple-element.374), channel_id=1, source_target_pairs={{0,16},{16,32},{32,48},{48,64},{64,80},{80,96},{96,112},{112,128},... | collective-permute-start | bytes 196616 | tf_op jit(solution)/shard_map/while/body/eval_jaxpr/ppermute | solution.py:29
  145.9 8.3 %collective-permute-start.1 = (bf16[256,128]{1,0:T(8,128)(2,1)S(1)}, bf16[256,128]{1,0:T(8,128)(2,1)S(1)}, u32[]{:S(2)}, u32[]{:S(2)}) collective-permute-start(bf16[256,128]{1,0:T(8,128)(2,1)S(1)} %get-tuple-element.375), channel_id=1, source_target_pairs={{0,16},{16,32},{32,48},{48,64},{64,80},{80,96},{96,112},{112,128},... | collective-permute-start | bytes 196616 | tf_op jit(solution)/shard_map/while/body/eval_jaxpr/ppermute | solution.py:29
  154.2 8.3 %collective-permute-start = (bf16[256,128]{1,0:T(8,128)(2,1)S(1)}, bf16[256,128]{1,0:T(8,128)(2,1)S(1)}, u32[]{:S(2)}, u32[]{:S(2)}) collective-permute-start(bf16[256,128]{1,0:T(8,128)(2,1)S(1)} %get-tuple-element.374), channel_id=1, source_target_pairs={{0,16},{16,32},{32,48},{48,64},{64,80},{80,96},{96,112},{112,128},... | collective-permute-start | bytes 196616 | tf_op jit(solution)/shard_map/while/body/eval_jaxpr/ppermute | solution.py:29
  156.1 8.3 %collective-permute-start.1 = (bf16[256,128]{1,0:T(8,128)(2,1)S(1)}, bf16[256,128]{1,0:T(8,128)(2,1)S(1)}, u32[]{:S(2)}, u32[]{:S(2)}) collective-permute-start(bf16[256,128]{1,0:T(8,128)(2,1)S(1)} %get-tuple-element.375), channel_id=1, source_target_pairs={{0,16},{16,32},{32,48},{48,64},{64,80},{80,96},{96,112},{112,128},... | collective-permute-start | bytes 196616 | tf_op jit(solution)/shard_map/while/body/eval_jaxpr/ppermute | solution.py:29
  164.5 8.3 %collective-permute-start = (bf16[256,128]{1,0:T(8,128)(2,1)S(1)}, bf16[256,128]{1,0:T(8,128)(2,1)S(1)}, u32[]{:S(2)}, u32[]{:S(2)}) collective-permute-start(bf16[256,128]{1,0:T(8,128)(2,1)S(1)} %get-tuple-element.374), channel_id=1, source_target_pairs={{0,16},{16,32},{32,48},{48,64},{64,80},{80,96},{96,112},{112,128},... | collective-permute-start | bytes 196616 | tf_op jit(solution)/shard_map/while/body/eval_jaxpr/ppermute | solution.py:29
  166.4 8.3 %collective-permute-start.1 = (bf16[256,128]{1,0:T(8,128)(2,1)S(1)}, bf16[256,128]{1,0:T(8,128)(2,1)S(1)}, u32[]{:S(2)}, u32[]{:S(2)}) collective-permute-start(bf16[256,128]{1,0:T(8,128)(2,1)S(1)} %get-tuple-element.375), channel_id=1, source_target_pairs={{0,16},{16,32},{32,48},{48,64},{64,80},{80,96},{96,112},{112,128},... | collective-permute-start | bytes 196616 | tf_op jit(solution)/shard_map/while/body/eval_jaxpr/ppermute | solution.py:29
  174.7 8.3 %collective-permute-start = (bf16[256,128]{1,0:T(8,128)(2,1)S(1)}, bf16[256,128]{1,0:T(8,128)(2,1)S(1)}, u32[]{:S(2)}, u32[]{:S(2)}) collective-permute-start(bf16[256,128]{1,0:T(8,128)(2,1)S(1)} %get-tuple-element.374), channel_id=1, source_target_pairs={{0,16},{16,32},{32,48},{48,64},{64,80},{80,96},{96,112},{112,128},... | collective-permute-start | bytes 196616 | tf_op jit(solution)/shard_map/while/body/eval_jaxpr/ppermute | solution.py:29
  176.6 8.3 %collective-permute-start.1 = (bf16[256,128]{1,0:T(8,128)(2,1)S(1)}, bf16[256,128]{1,0:T(8,128)(2,1)S(1)}, u32[]{:S(2)}, u32[]{:S(2)}) collective-permute-start(bf16[256,128]{1,0:T(8,128)(2,1)S(1)} %get-tuple-element.375), channel_id=1, source_target_pairs={{0,16},{16,32},{32,48},{48,64},{64,80},{80,96},{96,112},{112,128},... | collective-permute-start | bytes 196616 | tf_op jit(solution)/shard_map/while/body/eval_jaxpr/ppermute | solution.py:29
  210.1 139.5 %reduce-scatter.4.cloned.1.call-start = ((), (), s32[]{:S(2)}) async-start(), calls=%async_computation.5 | async-start | bytes 2785280
  225.2 6.7 %collective-permute-start.5 = (bf16[640,128]{1,0:T(8,128)(2,1)S(1)}, bf16[640,128]{1,0:T(8,128)(2,1)S(1)}, u32[]{:S(2)}, u32[]{:S(2)}) collective-permute-start(bf16[640,128]{1,0:T(8,128)(2,1)S(1)} %all_to_all.26), channel_id=1, source_target_pairs={{0,15},{1,0},{2,1},{3,2},{4,3},{5,4},{6,5},{7,6},{8,7},{9,8},{10,9... | collective-permute-start | bytes 491528 | tf_op jit(solution)/shard_map/ppermute | solution.py:19
  231.6 6.9 %collective-permute-start.6 = (bf16[640,128]{1,0:T(8,128)(2,1)S(1)}, bf16[640,128]{1,0:T(8,128)(2,1)S(1)}, u32[]{:S(2)}, u32[]{:S(2)}) collective-permute-start(bf16[640,128]{1,0:T(8,128)(2,1)S(1)} %collective-permute-done.4), channel_id=1, source_target_pairs={{0,1},{1,2},{2,3},{3,4},{4,5},{5,6},{6,7},{7,8},{8,9},{9,10},{10,1... | collective-permute-start | bytes 491528 | tf_op jit(solution)/shard_map/ppermute | solution.py:16
  231.9 6.7 %collective-permute-start.7 = (bf16[640,128]{1,0:T(8,128)(2,1)S(1)}, bf16[640,128]{1,0:T(8,128)(2,1)S(1)}, u32[]{:S(2)}, u32[]{:S(2)}) collective-permute-start(bf16[640,128]{1,0:T(8,128)(2,1)S(1)} %collective-permute-done.5), channel_id=1, source_target_pairs={{0,15},{1,0},{2,1},{3,2},{4,3},{5,4},{6,5},{7,6},{8,7},{9,8},{10,9... | collective-permute-start | bytes 491528 | tf_op jit(solution)/shard_map/ppermute | solution.py:19
  238.5 6.9 %collective-permute-start.8 = (bf16[640,128]{1,0:T(8,128)(2,1)S(1)}, bf16[640,128]{1,0:T(8,128)(2,1)S(1)}, u32[]{:S(2)}, u32[]{:S(2)}) collective-permute-start(bf16[640,128]{1,0:T(8,128)(2,1)S(1)} %collective-permute-done.6), channel_id=1, source_target_pairs={{0,1},{1,2},{2,3},{3,4},{4,5},{5,6},{6,7},{7,8},{8,9},{9,10},{10,1... | collective-permute-start | bytes 491528 | tf_op jit(solution)/shard_map/ppermute | solution.py:16
  238.5 6.9 %collective-permute-start.9 = (bf16[640,128]{1,0:T(8,128)(2,1)S(1)}, bf16[640,128]{1,0:T(8,128)(2,1)S(1)}, u32[]{:S(2)}, u32[]{:S(2)}) collective-permute-start(bf16[640,128]{1,0:T(8,128)(2,1)S(1)} %collective-permute-done.7), channel_id=1, source_target_pairs={{0,15},{1,0},{2,1},{3,2},{4,3},{5,4},{6,5},{7,6},{8,7},{9,8},{10,9... | collective-permute-start | bytes 491528 | tf_op jit(solution)/shard_map/ppermute | solution.py:19
  245.4 6.8 %collective-permute-start.10 = (bf16[640,128]{1,0:T(8,128)(2,1)S(1)}, bf16[640,128]{1,0:T(8,128)(2,1)S(1)}, u32[]{:S(2)}, u32[]{:S(2)}) collective-permute-start(bf16[640,128]{1,0:T(8,128)(2,1)S(1)} %collective-permute-done.8), channel_id=1, source_target_pairs={{0,1},{1,2},{2,3},{3,4},{4,5},{5,6},{6,7},{7,8},{8,9},{9,10},{10,1... | collective-permute-start | bytes 491528 | tf_op jit(solution)/shard_map/ppermute | solution.py:16
  245.4 6.8 %collective-permute-start.11 = (bf16[640,128]{1,0:T(8,128)(2,1)S(1)}, bf16[640,128]{1,0:T(8,128)(2,1)S(1)}, u32[]{:S(2)}, u32[]{:S(2)}) collective-permute-start(bf16[640,128]{1,0:T(8,128)(2,1)S(1)} %collective-permute-done.9), channel_id=1, source_target_pairs={{0,15},{1,0},{2,1},{3,2},{4,3},{5,4},{6,5},{7,6},{8,7},{9,8},{10,9... | collective-permute-start | bytes 491528 | tf_op jit(solution)/shard_map/ppermute | solution.py:19
  351.5 20.0 %all-to-all-start.2 = ((bf16[128,32,20]{0,2,1:T(8,128)(2,1)}), bf16[128,32,20]{0,2,1:T(8,128)(2,1)S(1)}, u32[]{:S(2)}, u32[]{:S(2)}) async-start(bf16[128,32,20]{0,2,1:T(8,128)(2,1)} %all_to_all.30), calls=%async_computation.2 | async-start | bytes 393216 | tf_op jit(solution)/shard_map/all_to_all | solution.py:146
  386.8 6.8 %collective-permute-start.2 = (bf16[256,128]{1,0:T(8,128)(2,1)S(1)}, bf16[256,128]{1,0:T(8,128)(2,1)S(1)}, u32[]{:S(2)}, u32[]{:S(2)}) collective-permute-start(bf16[256,128]{1,0:T(8,128)(2,1)S(1)} %get-tuple-element.397), channel_id=1, source_target_pairs={{16,0},{32,16},{48,32},{64,48},{80,64},{96,80},{112,96},{128,112},... | collective-permute-start | bytes 196616 | tf_op jit(solution)/shard_map/while/body/eval_jaxpr/ppermute | solution.py:29
  389.9 6.7 %collective-permute-start.3 = (bf16[256,128]{1,0:T(8,128)(2,1)S(1)}, bf16[256,128]{1,0:T(8,128)(2,1)S(1)}, u32[]{:S(2)}, u32[]{:S(2)}) collective-permute-start(bf16[256,128]{1,0:T(8,128)(2,1)S(1)} %get-tuple-element.398), channel_id=1, source_target_pairs={{16,0},{32,16},{48,32},{64,48},{80,64},{96,80},{112,96},{128,112},... | collective-permute-start | bytes 196616 | tf_op jit(solution)/shard_map/while/body/eval_jaxpr/ppermute | solution.py:29
  397.5 7.2 %collective-permute-start.2 = (bf16[256,128]{1,0:T(8,128)(2,1)S(1)}, bf16[256,128]{1,0:T(8,128)(2,1)S(1)}, u32[]{:S(2)}, u32[]{:S(2)}) collective-permute-start(bf16[256,128]{1,0:T(8,128)(2,1)S(1)} %get-tuple-element.397), channel_id=1, source_target_pairs={{16,0},{32,16},{48,32},{64,48},{80,64},{96,80},{112,96},{128,112},... | collective-permute-start | bytes 196616 | tf_op jit(solution)/shard_map/while/body/eval_jaxpr/ppermute | solution.py:29
  477.3 6.7 %collective-permute-start.2 = (bf16[256,128]{1,0:T(8,128)(2,1)S(1)}, bf16[256,128]{1,0:T(8,128)(2,1)S(1)}, u32[]{:S(2)}, u32[]{:S(2)}) collective-permute-start(bf16[256,128]{1,0:T(8,128)(2,1)S(1)} %get-tuple-element.397), channel_id=1, source_target_pairs={{16,0},{32,16},{48,32},{64,48},{80,64},{96,80},{112,96},{128,112},... | collective-permute-start | bytes 196616 | tf_op jit(solution)/shard_map/while/body/eval_jaxpr/ppermute | solution.py:29
  533.0 6.8 %collective-permute-start.2 = (bf16[256,128]{1,0:T(8,128)(2,1)S(1)}, bf16[256,128]{1,0:T(8,128)(2,1)S(1)}, u32[]{:S(2)}, u32[]{:S(2)}) collective-permute-start(bf16[256,128]{1,0:T(8,128)(2,1)S(1)} %get-tuple-element.397), channel_id=1, source_target_pairs={{16,0},{32,16},{48,32},{64,48},{80,64},{96,80},{112,96},{128,112},... | collective-permute-start | bytes 196616 | tf_op jit(solution)/shard_map/while/body/eval_jaxpr/ppermute | solution.py:29
  537.2 6.7 %collective-permute-start.3 = (bf16[256,128]{1,0:T(8,128)(2,1)S(1)}, bf16[256,128]{1,0:T(8,128)(2,1)S(1)}, u32[]{:S(2)}, u32[]{:S(2)}) collective-permute-start(bf16[256,128]{1,0:T(8,128)(2,1)S(1)} %get-tuple-element.398), channel_id=1, source_target_pairs={{16,0},{32,16},{48,32},{64,48},{80,64},{96,80},{112,96},{128,112},... | collective-permute-start | bytes 196616 | tf_op jit(solution)/shard_map/while/body/eval_jaxpr/ppermute | solution.py:29
  (46 other events, 535.7 us)
Sparse Core Ops, SparseCore 0:
  210.3 43.4 all-gather.1
  289.1 60.5 reduce-scatter.3
